TPU v7x, 256 devices: a whole 4x4x8 slice. The times are simulated.
256 devices in a mesh: row: 16 (over y, x), col: 16 (over z, core).
Axes of the slice: x: 4, y: 4, z: 8, core: 2. Of those that a mesh axis runs over, the one named last changes fastest.
Arguments:
- rhs: float32 [128, 32768], P('row', 'col'), may hold values from -60 to 60
- flex_tiles: float32 [131072, 2048], P('row', 'col'), may hold values from -0.25 to 0.25
- flex_cols: int32 [256, 64], P('row', 'col'), may hold values from 0 to 15, as said below
- stiff_tiles: float32 [131072, 2048], P('row', 'col'), may hold values from -0.25 to 0.25
- stiff_cols: int32 [256, 64], P('row', 'col'), may hold values from 0 to 15, as said below
- deflation: float32 [512, 32768], P('row', 'col'), may hold values from -0.375 to 0.375
- coarse_rows: float32 [8192, 8192], P(('row', 'col')), may hold values from -5 to 5, as said below
- face_rows: int32 [64, 2048], P('row', 'col'), may hold values from 0 to 2047, as said below
- face_len: int32 [16, 64], P('row', 'col'), may hold values from 0 to 128, as said below
Outputs:
- solution: float32 [128, 32768], P('row', 'col')
- residual: float32 [128, 32768], P('row', 'col')
- correction: float32 [128, 32768], P('row', 'col')
Inputs may be any that keep to these rules, and one draw needn't show every extreme that they name: `flex_cols`: row b of a subdomain's block list names 4 different block columns, the first being b. `stiff_cols`: row b of a subdomain's block list names 4 different block columns, the first being b. `coarse_rows`: the whole matrix is symmetric. `face_rows`: the four lists of a subdomain name 512 different multipliers of it. `face_len`: the two subdomains of a face give it the same length; faces on the grid's boundary have length 0, inner faces at least 32.
All inputs are finite; a program needn't handle non-finite values.
Results may differ from a plain program's by a relative error of at most 0.0003.
Values sent between devices are 32-bit elements; how exact they have to be, the bound alone decides.
A program may use at most 64 MiB of HBM per device.

v0:
```python
import jax
import jax.numpy as jnp
from jax import lax
from jax.sharding import PartitionSpec as P

ITERS = 3
PRECISE = lax.Precision.HIGHEST


def with_halo(cells, sides, width):
    for axis, dim in sides:
        count = lax.axis_size(axis)
        ends = count - 1
        head = lax.slice_in_dim(cells, 0, width, axis=dim)
        tail = lax.slice_in_dim(cells, cells.shape[dim] - width, cells.shape[dim], axis=dim)
        cells = jnp.concatenate(
            [
                lax.ppermute(tail, axis, [(i, (i + 1) % count) for i in range(ends)]),
                cells,
                lax.ppermute(head, axis, [((i + 1) % count, i) for i in range(ends)]),
            ],
            axis=dim,
        )
    return cells


def sparse_forward(vector, tile_set, columns):
    load_count = vector.shape[0]
    blocks, per_row = columns.shape
    tile_width = tile_set.shape[-1]
    pieces = vector.reshape(load_count, blocks, tile_width)
    picked = jnp.take(pieces, columns.reshape(-1), axis=1).reshape(
        load_count, blocks, per_row, tile_width
    )
    product = jnp.einsum("lbkw,bkwv->lbv", picked, tile_set, precision=PRECISE)
    return product.reshape(load_count, blocks * tile_width)


def sparse_backward(vector, tile_set, columns):
    load_count = vector.shape[0]
    blocks, per_row = columns.shape
    tile_width = tile_set.shape[-1]
    pieces = vector.reshape(load_count, blocks, tile_width)
    product = jnp.einsum("lbv,bkwv->lbkw", pieces, tile_set, precision=PRECISE)
    onehot = (columns[:, :, None] == jnp.arange(blocks, dtype=jnp.int32)[None, None, :]).astype(
        jnp.float32
    )
    summed = jnp.einsum("lbkw,bkj->ljw", product, onehot, precision=PRECISE)
    return summed.reshape(load_count, blocks * tile_width)


def pair_totals(first_field, second_field, third_field, fourth_field):
    return lax.psum(
        (jnp.sum(first_field * second_field, axis=1), jnp.sum(third_field * fourth_field, axis=1)),
        ("row", "col"),
    )


def shards(
    rhs, flex_tiles, flex_cols, stiff_tiles, stiff_cols, deflation, coarse_rows, face_rows, face_len
):
    blocks, per_row = flex_cols.shape
    tile_width = flex_tiles.shape[1]
    flex_set = flex_tiles.reshape(blocks, per_row, tile_width, tile_width)
    stiff_set = stiff_tiles.reshape(blocks, per_row, tile_width, tile_width)
    face_width = face_rows.shape[1]
    flat_index = face_rows.reshape(-1)
    slots = jnp.arange(face_width, dtype=jnp.int32)
    live_mask = (slots[None, :] < face_len.reshape(4, 1)).astype(jnp.float32)

    def face_part(vector):
        load_count = vector.shape[0]
        traces = jnp.take(vector, flat_index, axis=1).reshape(load_count, 4, face_width)
        across_rows = with_halo(traces[:, 0:2], (("row", 1),), 1)
        across_cols = with_halo(traces[:, 2:4], (("col", 1),), 1)
        partner = jnp.stack(
            [across_rows[:, 0], across_rows[:, 3], across_cols[:, 0], across_cols[:, 3]], axis=1
        )
        jump_values = (traces - partner) * live_mask[None]
        return (
            jnp.zeros_like(vector)
            .at[:, flat_index]
            .add(jump_values.reshape(load_count, 4 * face_width))
        )

    def operate(vector):
        coupling = face_part(vector)
        after_flex = sparse_forward(vector, flex_set, flex_cols)
        after_stiff = sparse_forward(after_flex, stiff_set, stiff_cols)
        back_stiff = sparse_backward(after_stiff, stiff_set, stiff_cols)
        local_part = sparse_backward(back_stiff, flex_set, flex_cols)
        return vector + local_part + coupling

    def precondition(vector):
        coefficients = jnp.einsum("lm,dm->ld", vector, deflation, precision=PRECISE)
        energy = jnp.einsum(
            "ln,dn->ld",
            lax.all_gather(coefficients, ("row", "col"), axis=1, tiled=True),
            coarse_rows,
            precision=PRECISE,
        )
        return vector + jnp.einsum("ld,dm->lm", energy, deflation, precision=PRECISE)

    residual = rhs
    solution = jnp.zeros_like(rhs)
    correction = precondition(residual)
    direction = correction
    image = operate(direction)
    curvature_sum, descent_sum = pair_totals(direction, image, residual, direction)
    for iteration in range(ITERS):
        step_size = (descent_sum / curvature_sum)[:, None]
        solution = solution + step_size * direction
        residual = residual - step_size * image
        correction = precondition(residual)
        if iteration + 1 < ITERS:
            cross_sum = lax.psum(jnp.sum(correction * image, axis=1), ("row", "col"))
            blend = -cross_sum / curvature_sum
            direction = correction + blend[:, None] * direction
            image = operate(direction)
            curvature_sum, descent_sum = pair_totals(direction, image, residual, direction)
    return (solution, residual, correction)


def solution(mesh):
    return jax.shard_map(
        shards,
        mesh=mesh,
        in_specs=(
            P("row", "col"),
            P("row", "col"),
            P("row", "col"),
            P("row", "col"),
            P("row", "col"),
            P("row", "col"),
            P(("row", "col"), None),
            P("row", "col"),
            P("row", "col"),
        ),
        out_specs=(P("row", "col"), P("row", "col"), P("row", "col")),
        check_vma=False,
    )
```

profile of v0, /device:TPU:1, one launch (start us, length us, event | category | flops | bytes accessed | tf_op | source)
XLA Modules:
  0.0 747.8 jit_solution(5366016694959184341)
XLA Ops:
  3.4 67.8 %all-gather = f32[256,32,8]{1,2,0:T(8,128)S(1)} all-gather(f32[1,32,8]{1,2,0:T(8,128)S(1)} %convolution_bitcast_fusion.21), channel_id=1, replica_groups=mesh['row'=16,'col'=16] {'row','col'}, dimensions={0}, use_global_device_ids=true | all-gather | bytes 263168 | tf_op jit(solution)/shard_map/all_gather | solution.py:98
  74.7 2.6 collective-permute-start
  78.8 1.9 collective-permute-start.2
  80.8 2.7 collective-permute-start.3
  84.8 3.8 convolution_bitcast_fusion.17
  89.4 4.0 convolution_bitcast_fusion.16
  93.5 3.6 convolution_bitcast_fusion.5
  97.4 3.6 convolution_bitcast_fusion.4
  102.2 4.2 scatter_custom_fusion
  106.9 78.0 %all-reduce.2 = (f32[8]{0:T(128)S(1)}, f32[8]{0:T(128)S(1)}) all-reduce(f32[8]{0:T(128)S(1)} %get-tuple-element.10, f32[8]{0:T(128)S(1)} %get-tuple-element.9), channel_id=1, replica_groups=mesh['row'=16,'col'=16] {'row','col'}, use_global_device_ids=true, to_apply=%region_1.2 | all-reduce | flops 16 | bytes 128 | tf_op jit(solution)/shard_map/psum | solution.py:53
  185.2 60.6 %all-gather.1 = f32[256,32,8]{1,2,0:T(8,128)S(1)} all-gather(f32[1,32,8]{1,2,0:T(8,128)S(1)} %convolution_bitcast_fusion.20), channel_id=1, replica_groups=mesh['row'=16,'col'=16] {'row','col'}, dimensions={0}, use_global_device_ids=true | all-gather | bytes 263168 | tf_op jit(solution)/shard_map/all_gather | solution.py:98
  247.8 75.0 %psum.58 = f32[8]{0:T(128)S(1)} all-reduce(f32[8]{0:T(128)S(1)} %get-tuple-element.31), channel_id=1, replica_groups=mesh['row'=16,'col'=16] {'row','col'}, use_global_device_ids=true, to_apply=%region_6.9 | all-reduce | flops 8 | bytes 64 | tf_op jit(solution)/shard_map/psum | solution.py:116
  327.5 4.5 collective-permute-start.6
  332.1 2.1 collective-permute-start.7
  335.0 3.8 convolution_bitcast_fusion.15
  339.7 4.0 convolution_bitcast_fusion.14
  343.7 3.6 convolution_bitcast_fusion.3
  347.6 3.6 convolution_bitcast_fusion.2
  352.4 3.9 scatter_custom_fusion.1
  356.8 77.0 %all-reduce.1 = (f32[8]{0:T(128)S(1)}, f32[8]{0:T(128)S(1)}) all-reduce(f32[8]{0:T(128)S(1)} %get-tuple-element.8, f32[8]{0:T(128)S(1)} %get-tuple-element.7), channel_id=1, replica_groups=mesh['row'=16,'col'=16] {'row','col'}, use_global_device_ids=true, to_apply=%region_8.11 | all-reduce | flops 16 | bytes 128 | tf_op jit(solution)/shard_map/psum | solution.py:53
  434.1 61.9 %all-gather.2 = f32[256,32,8]{1,2,0:T(8,128)S(1)} all-gather(f32[1,32,8]{1,2,0:T(8,128)S(1)} %convolution_bitcast_fusion.19), channel_id=1, replica_groups=mesh['row'=16,'col'=16] {'row','col'}, dimensions={0}, use_global_device_ids=true | all-gather | bytes 263168 | tf_op jit(solution)/shard_map/all_gather | solution.py:98
  498.0 73.7 %psum.61 = f32[8]{0:T(128)S(1)} all-reduce(f32[8]{0:T(128)S(1)} %get-tuple-element.33), channel_id=1, replica_groups=mesh['row'=16,'col'=16] {'row','col'}, use_global_device_ids=true, to_apply=%region_13.16 | all-reduce | flops 8 | bytes 64 | tf_op jit(solution)/shard_map/psum | solution.py:116
  573.4 3.8 collective-permute-start.10
  577.3 1.9 collective-permute-start.11
  579.2 2.0 collective-permute-start.8
  583.8 3.8 convolution_bitcast_fusion.13
  588.4 4.0 convolution_bitcast_fusion.12
  592.4 3.6 convolution_bitcast_fusion.1
  596.4 3.6 convolution_bitcast_fusion
  601.1 3.9 scatter_custom_fusion.2
  605.5 77.2 %all-reduce = (f32[8]{0:T(128)S(1)}, f32[8]{0:T(128)S(1)}) all-reduce(f32[8]{0:T(128)S(1)} %get-tuple-element.6, f32[8]{0:T(128)S(1)} %get-tuple-element.5), channel_id=1, replica_groups=mesh['row'=16,'col'=16] {'row','col'}, use_global_device_ids=true, to_apply=%region_15.18 | all-reduce | flops 16 | bytes 128 | tf_op jit(solution)/shard_map/psum | solution.py:53
  683.7 61.3 %all-gather.3 = f32[256,32,8]{1,2,0:T(8,128)S(1)} all-gather(f32[1,32,8]{1,2,0:T(8,128)S(1)} %convolution_bitcast_fusion.18), channel_id=1, replica_groups=mesh['row'=16,'col'=16] {'row','col'}, dimensions={0}, use_global_device_ids=true | all-gather | bytes 263168 | tf_op jit(solution)/shard_map/all_gather | solution.py:98
  (153 shorter events, 35.0 us)
Async XLA Ops:
  0.6 71.3 %copy-start = (f32[32,8192]{1,0:T(8,128)S(1)}, f32[32,8192]{1,0:T(8,128)}, u32[]{:S(2)}) copy-start(f32[32,8192]{1,0:T(8,128)} %param.19) | copy-start | bytes 3145732
  0.6 72.2 %copy-start.8 = (f32[8,2048]{1,0:T(8,128)S(1)}, f32[8,2048]{1,0:T(8,128)}, u32[]{:S(2)}) copy-start(f32[8,2048]{1,0:T(8,128)} %param.13) | copy-start | bytes 196612
  0.7 72.2 %copy-start.7 = (f32[32,2048]{1,0:T(8,128)S(1)}, f32[32,2048]{1,0:T(8,128)}, u32[]{:S(2)}) copy-start(f32[32,2048]{1,0:T(8,128)} %param.18) | copy-start | bytes 786436
  3.4 80.1 %copy-start.11 = (s32[16,4]{0,1:T(4,128)S(1)}, s32[16,4]{0,1:T(4,128)}, u32[]{:S(2)}) copy-start(s32[16,4]{0,1:T(4,128)} %param.15) | copy-start | bytes 772
  3.4 80.3 %copy-start.10 = (s32[16,4]{0,1:T(4,128)S(1)}, s32[16,4]{0,1:T(4,128)}, u32[]{:S(2)}) copy-start(s32[16,4]{0,1:T(4,128)} %param.17) | copy-start | bytes 772
  3.4 80.5 %copy-start.13 = (s32[1,4]{1,0:T(1,128)S(1)}, s32[1,4]{1,0:T(1,128)}, u32[]{:S(2)}) copy-start(s32[1,4]{1,0:T(1,128)} %param.21) | copy-start | bytes 52
  74.7 27.1 %collective-permute-start = (f32[8,1,128]{2,0,1:T(8,128)S(1)}, f32[8,1,128]{2,0,1:T(8,128)S(1)}, u32[]{:S(2)}, u32[]{:S(2)}) collective-permute-start(f32[8,1,128]{2,0,1:T(8,128)S(1)} %copy.118), channel_id=1, source_target_pairs={{0,16},{16,32},{32,48},{48,64},{64,80},{80,96},{96,112},{112,128},... | collective-permute-start | bytes 12296 | tf_op jit(solution)/shard_map/ppermute | solution.py:18
  77.4 24.4 %collective-permute-start.1 = (f32[8,1,128]{2,0,1:T(8,128)S(1)}, f32[8,1,128]{2,0,1:T(8,128)S(1)}, u32[]{:S(2)}, u32[]{:S(2)}) collective-permute-start(f32[8,1,128]{2,0,1:T(8,128)S(1)} %copy.119), channel_id=1, source_target_pairs={{16,0},{32,16},{48,32},{64,48},{80,64},{96,80},{112,96},{128,112},... | collective-permute-start | bytes 12296 | tf_op jit(solution)/shard_map/ppermute | solution.py:20
  78.8 23.0 %collective-permute-start.2 = (f32[8,1,128]{2,0,1:T(8,128)S(1)}, f32[8,1,128]{2,0,1:T(8,128)S(1)}, u32[]{:S(2)}, u32[]{:S(2)}) collective-permute-start(f32[8,1,128]{2,0,1:T(8,128)S(1)} %copy.120), channel_id=1, source_target_pairs={{0,1},{1,2},{2,3},{3,4},{4,5},{5,6},{6,7},{7,8},{8,9},{9,10},{10,1... | collective-permute-start | bytes 12296 | tf_op jit(solution)/shard_map/ppermute | solution.py:18
  80.8 21.1 %collective-permute-start.3 = (f32[8,1,128]{2,0,1:T(8,128)S(1)}, f32[8,1,128]{2,0,1:T(8,128)S(1)}, u32[]{:S(2)}, u32[]{:S(2)}) collective-permute-start(f32[8,1,128]{2,0,1:T(8,128)S(1)} %copy.121), channel_id=1, source_target_pairs={{1,0},{2,1},{3,2},{4,3},{5,4},{6,5},{7,6},{8,7},{9,8},{10,9},{11,1... | collective-permute-start | bytes 12296 | tf_op jit(solution)/shard_map/ppermute | solution.py:20
  89.3 4.2 copy-start.1
  89.4 8.0 %copy-start.4 = (f32[8192,128]{1,0:T(8,128)S(1)}, f32[8192,128]{1,0:T(8,128)}, u32[]{:S(2)}) copy-start(f32[8192,128]{1,0:T(8,128)} %param.14) | copy-start | bytes 12582916
  93.4 8.0 %copy-start.12 = (s32[4,128]{1,0:T(4,128)S(1)}, s32[4,128]{1,0:T(4,128)}, u32[]{:S(2)}) copy-start(s32[4,128]{1,0:T(4,128)} %param.20) | copy-start | bytes 6148
  324.6 27.4 %collective-permute-start.4 = (f32[8,1,128]{2,0,1:T(8,128)S(1)}, f32[8,1,128]{2,0,1:T(8,128)S(1)}, u32[]{:S(2)}, u32[]{:S(2)}) collective-permute-start(f32[8,1,128]{2,0,1:T(8,128)S(1)} %copy.122), channel_id=1, source_target_pairs={{0,16},{16,32},{32,48},{48,64},{64,80},{80,96},{96,112},{112,128},... | collective-permute-start | bytes 12296 | tf_op jit(solution)/shard_map/ppermute | solution.py:18
  326.2 25.8 %collective-permute-start.5 = (f32[8,1,128]{2,0,1:T(8,128)S(1)}, f32[8,1,128]{2,0,1:T(8,128)S(1)}, u32[]{:S(2)}, u32[]{:S(2)}) collective-permute-start(f32[8,1,128]{2,0,1:T(8,128)S(1)} %copy.123), channel_id=1, source_target_pairs={{16,0},{32,16},{48,32},{64,48},{80,64},{96,80},{112,96},{128,112},... | collective-permute-start | bytes 12296 | tf_op jit(solution)/shard_map/ppermute | solution.py:20
  327.5 24.5 %collective-permute-start.6 = (f32[8,1,128]{2,0,1:T(8,128)S(1)}, f32[8,1,128]{2,0,1:T(8,128)S(1)}, u32[]{:S(2)}, u32[]{:S(2)}) collective-permute-start(f32[8,1,128]{2,0,1:T(8,128)S(1)} %copy.124), channel_id=1, source_target_pairs={{0,1},{1,2},{2,3},{3,4},{4,5},{5,6},{6,7},{7,8},{8,9},{9,10},{10,1... | collective-permute-start | bytes 12296 | tf_op jit(solution)/shard_map/ppermute | solution.py:18
  332.1 19.9 %collective-permute-start.7 = (f32[8,1,128]{2,0,1:T(8,128)S(1)}, f32[8,1,128]{2,0,1:T(8,128)S(1)}, u32[]{:S(2)}, u32[]{:S(2)}) collective-permute-start(f32[8,1,128]{2,0,1:T(8,128)S(1)} %copy.125), channel_id=1, source_target_pairs={{1,0},{2,1},{3,2},{4,3},{5,4},{6,5},{7,6},{8,7},{9,8},{10,9},{11,1... | collective-permute-start | bytes 12296 | tf_op jit(solution)/shard_map/ppermute | solution.py:20
  339.5 4.2 copy-start.2
  339.6 8.0 %copy-start.5 = (f32[8192,128]{1,0:T(8,128)S(1)}, f32[8192,128]{1,0:T(8,128)}, u32[]{:S(2)}) copy-start(f32[8192,128]{1,0:T(8,128)} %param.14) | copy-start | bytes 12582916
  573.4 27.4 %collective-permute-start.10 = (f32[8,1,128]{2,0,1:T(8,128)S(1)}, f32[8,1,128]{2,0,1:T(8,128)S(1)}, u32[]{:S(2)}, u32[]{:S(2)}) collective-permute-start(f32[8,1,128]{2,0,1:T(8,128)S(1)} %copy.128), channel_id=1, source_target_pairs={{0,1},{1,2},{2,3},{3,4},{4,5},{5,6},{6,7},{7,8},{8,9},{9,10},{10,1... | collective-permute-start | bytes 12296 | tf_op jit(solution)/shard_map/ppermute | solution.py:18
  577.3 23.5 %collective-permute-start.11 = (f32[8,1,128]{2,0,1:T(8,128)S(1)}, f32[8,1,128]{2,0,1:T(8,128)S(1)}, u32[]{:S(2)}, u32[]{:S(2)}) collective-permute-start(f32[8,1,128]{2,0,1:T(8,128)S(1)} %copy.129), channel_id=1, source_target_pairs={{1,0},{2,1},{3,2},{4,3},{5,4},{6,5},{7,6},{8,7},{9,8},{10,9},{11,1... | collective-permute-start | bytes 12296 | tf_op jit(solution)/shard_map/ppermute | solution.py:20
  579.2 21.5 %collective-permute-start.8 = (f32[8,1,128]{2,0,1:T(8,128)S(1)}, f32[8,1,128]{2,0,1:T(8,128)S(1)}, u32[]{:S(2)}, u32[]{:S(2)}) collective-permute-start(f32[8,1,128]{2,0,1:T(8,128)S(1)} %copy.126), channel_id=1, source_target_pairs={{0,16},{16,32},{32,48},{48,64},{64,80},{80,96},{96,112},{112,128},... | collective-permute-start | bytes 12296 | tf_op jit(solution)/shard_map/ppermute | solution.py:18
  581.3 19.5 %collective-permute-start.9 = (f32[8,1,128]{2,0,1:T(8,128)S(1)}, f32[8,1,128]{2,0,1:T(8,128)S(1)}, u32[]{:S(2)}, u32[]{:S(2)}) collective-permute-start(f32[8,1,128]{2,0,1:T(8,128)S(1)} %copy.127), channel_id=1, source_target_pairs={{16,0},{32,16},{48,32},{64,48},{80,64},{96,80},{112,96},{128,112},... | collective-permute-start | bytes 12296 | tf_op jit(solution)/shard_map/ppermute | solution.py:20
  588.2 4.2 copy-start.3
  588.4 8.0 %copy-start.6 = (f32[8192,128]{1,0:T(8,128)S(1)}, f32[8192,128]{1,0:T(8,128)}, u32[]{:S(2)}) copy-start(f32[8192,128]{1,0:T(8,128)} %param.14) | copy-start | bytes 12582916
  683.5 64.1 %copy-start.9 = (f32[8,2048]{1,0:T(8,128)}, f32[8,2048]{1,0:T(8,128)S(1)}, u32[]{:S(2)}) copy-start(f32[8,2048]{1,0:T(8,128)S(1)} %get-tuple-element.29) | copy-start | bytes 196612
where the time goes:
time: 753 us; the launch traced here: 748 us
  blocking collectives  633 us (84%)
  matrix products  54.8 us (7%)
  starting transfers between devices  27.5 us (4%)
  other arithmetic  17 us (2%)
  local copies, waits for them, and re-layouts  14.1 us (2%)
    all_gather x4, blocking collectives, precondition(): lax.all_gather(coefficients, ('row', 'col'), axis=1, tiled=True)  252 us
    psum x3, blocking collectives, pair_totals(): lax.psum((jnp.sum(first_field * second_field, axis=1), jnp.sum(third_fiel...  232 us
    psum x2, blocking collectives, shards(): cross_sum = lax.psum(jnp.sum(correction * image, axis=1), ('row', 'col'))  149 us
    dot_general x6, matrix products, sparse_forward(): product = jnp.einsum('lbkw,bkwv->lbv', picked, tile_set, precision=PRECISE)  23.5 us
    dot_general x6, matrix products, sparse_backward(): product = jnp.einsum('lbv,bkwv->lbkw', pieces, tile_set, precision=PRECISE)  21.4 us
    ppermute x6, starting transfers between devices, with_halo(): lax.ppermute(tail, axis, [(i, (i + 1) % count) for i in range(ends)])  16.4 us
  transfers between devices with their start and end apart: 12, of which 0 were waited for; matrix products, arithmetic and copies ran while one was open for 7% of the time, Pallas kernels for 0%

commit v1 on v0

--- a/solution.py
+++ b/solution.py
@@ -51,8 +51,14 @@
 
 def pair_totals(first_field, second_field, third_field, fourth_field):
     return lax.psum(
-        (jnp.sum(first_field * second_field, axis=1), jnp.sum(third_field * fourth_field, axis=1)),
-        ("row", "col"),
+        lax.psum(
+            (
+                jnp.sum(first_field * second_field, axis=1),
+                jnp.sum(third_field * fourth_field, axis=1),
+            ),
+            "row",
+        ),
+        "col",
     )
 
 

time: 753 us -> 706 us (0.938)
  blocking collectives: 633 us -> 587 us
    psum x3, blocking collectives: 232 us -> 96.8 us  [pair_totals(): lax.psum((jnp.sum(first_field * second_field, axis=1), jnp.sum(third_fiel...]
    psum x0 -> x3, blocking collectives: none -> 91.3 us  [pair_totals(): lax.psum(lax.psum((jnp.sum(first_field * second_field, axis=1), jnp.sum(t...]
  transfers between devices with their start and end apart: 12 -> 12, of which waited for: 0 -> 0; matrix products, arithmetic and copies ran while one was open for 7% -> 8% of each run, Pallas kernels for 0% -> 0%
where the time goes in v1:
time: 706 us; the launch traced here: 701 us
  blocking collectives  587 us (83%)
  matrix products  54.8 us (8%)
  starting transfers between devices  26.6 us (4%)
  other arithmetic  16.8 us (2%)
  local copies, waits for them, and re-layouts  14.1 us (2%)
    all_gather x4, blocking collectives, precondition(): lax.all_gather(coefficients, ('row', 'col'), axis=1, tiled=True)  248 us
    psum x2, blocking collectives, shards(): cross_sum = lax.psum(jnp.sum(correction * image, axis=1), ('row', 'col'))  151 us
    psum x3, blocking collectives, pair_totals(): lax.psum((jnp.sum(first_field * second_field, axis=1), jnp.sum(third_fiel...  96.8 us
    psum x3, blocking collectives, pair_totals(): lax.psum(lax.psum((jnp.sum(first_field * second_field, axis=1), jnp.sum(t...  91.3 us
    dot_general x6, matrix products, sparse_forward(): product = jnp.einsum('lbkw,bkwv->lbv', picked, tile_set, precision=PRECISE)  23.5 us
    dot_general x6, matrix products, sparse_backward(): product = jnp.einsum('lbv,bkwv->lbkw', pieces, tile_set, precision=PRECISE)  21.4 us
    ppermute x6, starting transfers between devices, with_halo(): lax.ppermute(tail, axis, [(i, (i + 1) % count) for i in range(ends)])  15.5 us
  transfers between devices with their start and end apart: 12, of which 0 were waited for; matrix products, arithmetic and copies ran while one was open for 8% of the time, Pallas kernels for 0%

profile of v1, /device:TPU:1, one launch (start us, length us, event | category | flops | bytes accessed | tf_op | source)
XLA Modules:
  0.0 700.6 jit_solution(5585549352057208321)
XLA Ops:
  3.4 67.8 %all-gather = f32[256,32,8]{1,2,0:T(8,128)S(1)} all-gather(f32[1,32,8]{1,2,0:T(8,128)S(1)} %convolution_bitcast_fusion.21), channel_id=1, replica_groups=mesh['row'=16,'col'=16] {'row','col'}, dimensions={0}, use_global_device_ids=true | all-gather | bytes 263168 | tf_op jit(solution)/shard_map/all_gather | solution.py:104
  74.7 2.6 collective-permute-start
  80.8 2.6 collective-permute-start.3
  84.7 3.8 convolution_bitcast_fusion.17
  89.3 4.0 convolution_bitcast_fusion.16
  93.3 3.6 convolution_bitcast_fusion.5
  97.3 3.6 convolution_bitcast_fusion.4
  102.1 3.9 scatter_custom_fusion
  106.5 32.2 %all-reduce.5 = (f32[8]{0:T(128)S(1)}, f32[8]{0:T(128)S(1)}) all-reduce(f32[8]{0:T(128)S(1)} %get-tuple-element.10, f32[8]{0:T(128)S(1)} %get-tuple-element.9), channel_id=1, replica_groups=mesh['row'=16,'col'=16] {'row'}, use_global_device_ids=true, to_apply=%region_1.2 | all-reduce | flops 16 | bytes 128 | tf_op jit(solution)/shard_map/psum | solution.py:54
  138.7 30.1 %all-reduce.2 = (f32[8]{0:T(128)S(1)}, f32[8]{0:T(128)S(1)}) all-reduce(f32[8]{0:T(128)S(1)} %get-tuple-element.21, f32[8]{0:T(128)S(1)} %get-tuple-element.22), channel_id=1, replica_groups=mesh['row'=16,'col'=16] {'col'}, use_global_device_ids=true, to_apply=%region_2.3 | all-reduce | flops 16 | bytes 128 | tf_op jit(solution)/shard_map/psum | solution.py:53
  169.2 59.8 %all-gather.1 = f32[256,32,8]{1,2,0:T(8,128)S(1)} all-gather(f32[1,32,8]{1,2,0:T(8,128)S(1)} %convolution_bitcast_fusion.20), channel_id=1, replica_groups=mesh['row'=16,'col'=16] {'row','col'}, dimensions={0}, use_global_device_ids=true | all-gather | bytes 263168 | tf_op jit(solution)/shard_map/all_gather | solution.py:104
  230.9 75.4 %psum.102 = f32[8]{0:T(128)S(1)} all-reduce(f32[8]{0:T(128)S(1)} %get-tuple-element.37), channel_id=1, replica_groups=mesh['row'=16,'col'=16] {'row','col'}, use_global_device_ids=true, to_apply=%region_8.11 | all-reduce | flops 8 | bytes 64 | tf_op jit(solution)/shard_map/psum | solution.py:122
  308.1 3.2 collective-permute-start.4
  314.9 2.7 collective-permute-start.7
  318.3 3.8 convolution_bitcast_fusion.15
  323.0 4.0 convolution_bitcast_fusion.14
  327.0 3.6 convolution_bitcast_fusion.3
  330.9 3.6 convolution_bitcast_fusion.2
  335.7 3.9 scatter_custom_fusion.1
  340.0 32.3 %all-reduce.4 = (f32[8]{0:T(128)S(1)}, f32[8]{0:T(128)S(1)}) all-reduce(f32[8]{0:T(128)S(1)} %get-tuple-element.8, f32[8]{0:T(128)S(1)} %get-tuple-element.7), channel_id=1, replica_groups=mesh['row'=16,'col'=16] {'row'}, use_global_device_ids=true, to_apply=%region_10.13 | all-reduce | flops 16 | bytes 128 | tf_op jit(solution)/shard_map/psum | solution.py:54
  372.3 30.6 %all-reduce.1 = (f32[8]{0:T(128)S(1)}, f32[8]{0:T(128)S(1)}) all-reduce(f32[8]{0:T(128)S(1)} %get-tuple-element.19, f32[8]{0:T(128)S(1)} %get-tuple-element.20), channel_id=1, replica_groups=mesh['row'=16,'col'=16] {'col'}, use_global_device_ids=true, to_apply=%region_11.14 | all-reduce | flops 16 | bytes 128 | tf_op jit(solution)/shard_map/psum | solution.py:53
  403.3 60.0 %all-gather.2 = f32[256,32,8]{1,2,0:T(8,128)S(1)} all-gather(f32[1,32,8]{1,2,0:T(8,128)S(1)} %convolution_bitcast_fusion.19), channel_id=1, replica_groups=mesh['row'=16,'col'=16] {'row','col'}, dimensions={0}, use_global_device_ids=true | all-gather | bytes 263168 | tf_op jit(solution)/shard_map/all_gather | solution.py:104
  465.3 75.4 %psum.107 = f32[8]{0:T(128)S(1)} all-reduce(f32[8]{0:T(128)S(1)} %get-tuple-element.39), channel_id=1, replica_groups=mesh['row'=16,'col'=16] {'row','col'}, use_global_device_ids=true, to_apply=%region_17.20 | all-reduce | flops 8 | bytes 64 | tf_op jit(solution)/shard_map/psum | solution.py:122
  542.4 4.0 collective-permute-start.10
  552.2 3.8 convolution_bitcast_fusion.13
  556.8 4.0 convolution_bitcast_fusion.12
  560.8 3.6 convolution_bitcast_fusion.1
  564.8 3.6 convolution_bitcast_fusion
  569.6 3.9 scatter_custom_fusion.2
  573.9 32.3 %all-reduce.3 = (f32[8]{0:T(128)S(1)}, f32[8]{0:T(128)S(1)}) all-reduce(f32[8]{0:T(128)S(1)} %get-tuple-element.6, f32[8]{0:T(128)S(1)} %get-tuple-element.5), channel_id=1, replica_groups=mesh['row'=16,'col'=16] {'row'}, use_global_device_ids=true, to_apply=%region_19.22 | all-reduce | flops 16 | bytes 128 | tf_op jit(solution)/shard_map/psum | solution.py:54
  606.3 30.6 %all-reduce = (f32[8]{0:T(128)S(1)}, f32[8]{0:T(128)S(1)}) all-reduce(f32[8]{0:T(128)S(1)} %get-tuple-element.17, f32[8]{0:T(128)S(1)} %get-tuple-element.18), channel_id=1, replica_groups=mesh['row'=16,'col'=16] {'col'}, use_global_device_ids=true, to_apply=%region_20.23 | all-reduce | flops 16 | bytes 128 | tf_op jit(solution)/shard_map/psum | solution.py:53
  637.8 60.0 %all-gather.3 = f32[256,32,8]{1,2,0:T(8,128)S(1)} all-gather(f32[1,32,8]{1,2,0:T(8,128)S(1)} %convolution_bitcast_fusion.18), channel_id=1, replica_groups=mesh['row'=16,'col'=16] {'row','col'}, dimensions={0}, use_global_device_ids=true | all-gather | bytes 263168 | tf_op jit(solution)/shard_map/all_gather | solution.py:104
  (156 shorter events, 40.6 us)
Async XLA Ops:
  0.6 71.3 %copy-start = (f32[32,8192]{1,0:T(8,128)S(1)}, f32[32,8192]{1,0:T(8,128)}, u32[]{:S(2)}) copy-start(f32[32,8192]{1,0:T(8,128)} %param.19) | copy-start | bytes 3145732
  0.6 72.2 %copy-start.8 = (f32[8,2048]{1,0:T(8,128)S(1)}, f32[8,2048]{1,0:T(8,128)}, u32[]{:S(2)}) copy-start(f32[8,2048]{1,0:T(8,128)} %param.13) | copy-start | bytes 196612
  0.7 72.2 %copy-start.7 = (f32[32,2048]{1,0:T(8,128)S(1)}, f32[32,2048]{1,0:T(8,128)}, u32[]{:S(2)}) copy-start(f32[32,2048]{1,0:T(8,128)} %param.18) | copy-start | bytes 786436
  3.4 80.0 %copy-start.11 = (s32[16,4]{0,1:T(4,128)S(1)}, s32[16,4]{0,1:T(4,128)}, u32[]{:S(2)}) copy-start(s32[16,4]{0,1:T(4,128)} %param.15) | copy-start | bytes 772
  3.4 80.2 %copy-start.10 = (s32[16,4]{0,1:T(4,128)S(1)}, s32[16,4]{0,1:T(4,128)}, u32[]{:S(2)}) copy-start(s32[16,4]{0,1:T(4,128)} %param.17) | copy-start | bytes 772
  3.4 80.4 %copy-start.13 = (s32[1,4]{1,0:T(1,128)S(1)}, s32[1,4]{1,0:T(1,128)}, u32[]{:S(2)}) copy-start(s32[1,4]{1,0:T(1,128)} %param.21) | copy-start | bytes 52
  74.7 27.0 %collective-permute-start = (f32[8,1,128]{2,0,1:T(8,128)S(1)}, f32[8,1,128]{2,0,1:T(8,128)S(1)}, u32[]{:S(2)}, u32[]{:S(2)}) collective-permute-start(f32[8,1,128]{2,0,1:T(8,128)S(1)} %copy.118), channel_id=1, source_target_pairs={{0,16},{16,32},{32,48},{48,64},{64,80},{80,96},{96,112},{112,128},... | collective-permute-start | bytes 12296 | tf_op jit(solution)/shard_map/ppermute | solution.py:18
  77.4 24.3 %collective-permute-start.1 = (f32[8,1,128]{2,0,1:T(8,128)S(1)}, f32[8,1,128]{2,0,1:T(8,128)S(1)}, u32[]{:S(2)}, u32[]{:S(2)}) collective-permute-start(f32[8,1,128]{2,0,1:T(8,128)S(1)} %copy.119), channel_id=1, source_target_pairs={{16,0},{32,16},{48,32},{64,48},{80,64},{96,80},{112,96},{128,112},... | collective-permute-start | bytes 12296 | tf_op jit(solution)/shard_map/ppermute | solution.py:20
  78.8 22.9 %collective-permute-start.2 = (f32[8,1,128]{2,0,1:T(8,128)S(1)}, f32[8,1,128]{2,0,1:T(8,128)S(1)}, u32[]{:S(2)}, u32[]{:S(2)}) collective-permute-start(f32[8,1,128]{2,0,1:T(8,128)S(1)} %copy.120), channel_id=1, source_target_pairs={{0,1},{1,2},{2,3},{3,4},{4,5},{5,6},{6,7},{7,8},{8,9},{9,10},{10,1... | collective-permute-start | bytes 12296 | tf_op jit(solution)/shard_map/ppermute | solution.py:18
  80.8 20.9 %collective-permute-start.3 = (f32[8,1,128]{2,0,1:T(8,128)S(1)}, f32[8,1,128]{2,0,1:T(8,128)S(1)}, u32[]{:S(2)}, u32[]{:S(2)}) collective-permute-start(f32[8,1,128]{2,0,1:T(8,128)S(1)} %copy.121), channel_id=1, source_target_pairs={{1,0},{2,1},{3,2},{4,3},{5,4},{6,5},{7,6},{8,7},{9,8},{10,9},{11,1... | collective-permute-start | bytes 12296 | tf_op jit(solution)/shard_map/ppermute | solution.py:20
  89.2 4.2 copy-start.1
  89.3 8.0 %copy-start.4 = (f32[8192,128]{1,0:T(8,128)S(1)}, f32[8192,128]{1,0:T(8,128)}, u32[]{:S(2)}) copy-start(f32[8192,128]{1,0:T(8,128)} %param.14) | copy-start | bytes 12582916
  93.3 8.0 %copy-start.12 = (s32[4,128]{1,0:T(4,128)S(1)}, s32[4,128]{1,0:T(4,128)}, u32[]{:S(2)}) copy-start(s32[4,128]{1,0:T(4,128)} %param.20) | copy-start | bytes 6148
  308.1 27.2 %collective-permute-start.4 = (f32[8,1,128]{2,0,1:T(8,128)S(1)}, f32[8,1,128]{2,0,1:T(8,128)S(1)}, u32[]{:S(2)}, u32[]{:S(2)}) collective-permute-start(f32[8,1,128]{2,0,1:T(8,128)S(1)} %copy.122), channel_id=1, source_target_pairs={{0,16},{16,32},{32,48},{48,64},{64,80},{80,96},{96,112},{112,128},... | collective-permute-start | bytes 12296 | tf_op jit(solution)/shard_map/ppermute | solution.py:18
  311.3 24.0 %collective-permute-start.5 = (f32[8,1,128]{2,0,1:T(8,128)S(1)}, f32[8,1,128]{2,0,1:T(8,128)S(1)}, u32[]{:S(2)}, u32[]{:S(2)}) collective-permute-start(f32[8,1,128]{2,0,1:T(8,128)S(1)} %copy.123), channel_id=1, source_target_pairs={{16,0},{32,16},{48,32},{64,48},{80,64},{96,80},{112,96},{128,112},... | collective-permute-start | bytes 12296 | tf_op jit(solution)/shard_map/ppermute | solution.py:20
  312.7 22.7 %collective-permute-start.6 = (f32[8,1,128]{2,0,1:T(8,128)S(1)}, f32[8,1,128]{2,0,1:T(8,128)S(1)}, u32[]{:S(2)}, u32[]{:S(2)}) collective-permute-start(f32[8,1,128]{2,0,1:T(8,128)S(1)} %copy.124), channel_id=1, source_target_pairs={{0,1},{1,2},{2,3},{3,4},{4,5},{5,6},{6,7},{7,8},{8,9},{9,10},{10,1... | collective-permute-start | bytes 12296 | tf_op jit(solution)/shard_map/ppermute | solution.py:18
  314.9 20.5 %collective-permute-start.7 = (f32[8,1,128]{2,0,1:T(8,128)S(1)}, f32[8,1,128]{2,0,1:T(8,128)S(1)}, u32[]{:S(2)}, u32[]{:S(2)}) collective-permute-start(f32[8,1,128]{2,0,1:T(8,128)S(1)} %copy.125), channel_id=1, source_target_pairs={{1,0},{2,1},{3,2},{4,3},{5,4},{6,5},{7,6},{8,7},{9,8},{10,9},{11,1... | collective-permute-start | bytes 12296 | tf_op jit(solution)/shard_map/ppermute | solution.py:20
  322.8 4.2 copy-start.2
  323.0 8.0 %copy-start.5 = (f32[8192,128]{1,0:T(8,128)S(1)}, f32[8192,128]{1,0:T(8,128)}, u32[]{:S(2)}) copy-start(f32[8192,128]{1,0:T(8,128)} %param.14) | copy-start | bytes 12582916
  542.4 26.8 %collective-permute-start.10 = (f32[8,1,128]{2,0,1:T(8,128)S(1)}, f32[8,1,128]{2,0,1:T(8,128)S(1)}, u32[]{:S(2)}, u32[]{:S(2)}) collective-permute-start(f32[8,1,128]{2,0,1:T(8,128)S(1)} %copy.128), channel_id=1, source_target_pairs={{0,1},{1,2},{2,3},{3,4},{4,5},{5,6},{6,7},{7,8},{8,9},{9,10},{10,1... | collective-permute-start | bytes 12296 | tf_op jit(solution)/shard_map/ppermute | solution.py:18
  546.5 22.7 %collective-permute-start.11 = (f32[8,1,128]{2,0,1:T(8,128)S(1)}, f32[8,1,128]{2,0,1:T(8,128)S(1)}, u32[]{:S(2)}, u32[]{:S(2)}) collective-permute-start(f32[8,1,128]{2,0,1:T(8,128)S(1)} %copy.129), channel_id=1, source_target_pairs={{1,0},{2,1},{3,2},{4,3},{5,4},{6,5},{7,6},{8,7},{9,8},{10,9},{11,1... | collective-permute-start | bytes 12296 | tf_op jit(solution)/shard_map/ppermute | solution.py:20
  548.5 20.7 %collective-permute-start.8 = (f32[8,1,128]{2,0,1:T(8,128)S(1)}, f32[8,1,128]{2,0,1:T(8,128)S(1)}, u32[]{:S(2)}, u32[]{:S(2)}) collective-permute-start(f32[8,1,128]{2,0,1:T(8,128)S(1)} %copy.126), channel_id=1, source_target_pairs={{0,16},{16,32},{32,48},{48,64},{64,80},{80,96},{96,112},{112,128},... | collective-permute-start | bytes 12296 | tf_op jit(solution)/shard_map/ppermute | solution.py:18
  550.1 19.1 %collective-permute-start.9 = (f32[8,1,128]{2,0,1:T(8,128)S(1)}, f32[8,1,128]{2,0,1:T(8,128)S(1)}, u32[]{:S(2)}, u32[]{:S(2)}) collective-permute-start(f32[8,1,128]{2,0,1:T(8,128)S(1)} %copy.127), channel_id=1, source_target_pairs={{16,0},{32,16},{48,32},{64,48},{80,64},{96,80},{112,96},{128,112},... | collective-permute-start | bytes 12296 | tf_op jit(solution)/shard_map/ppermute | solution.py:20
  556.7 4.2 copy-start.3
  556.8 8.0 %copy-start.6 = (f32[8192,128]{1,0:T(8,128)S(1)}, f32[8192,128]{1,0:T(8,128)}, u32[]{:S(2)}) copy-start(f32[8192,128]{1,0:T(8,128)} %param.14) | copy-start | bytes 12582916
  637.6 62.8 %copy-start.9 = (f32[8,2048]{1,0:T(8,128)}, f32[8,2048]{1,0:T(8,128)S(1)}, u32[]{:S(2)}) copy-start(f32[8,2048]{1,0:T(8,128)S(1)} %get-tuple-element.35) | copy-start | bytes 196612
